TPU v7x, 32 devices: a whole 2x2x4 slice. The times are simulated.
32 devices in a mesh: dp: 16 (over z, x, core), head: 2 (over y).
Axes of the slice: x: 2, y: 2, z: 4, core: 2. Of those that a mesh axis runs over, the one named last changes fastest.
Arguments:
- tokens: bfloat16 [16384, 1024], P(('dp', 'head')), may hold values from -6 to 6
- lengths: int32 [16], P('dp'), may hold values from 128 to 1024, as said below
- decay: float32 [8], P('head'), may hold values from 0.00048828125 to 0.03125
- w_query: bfloat16 [1024, 1024], P(None, 'head'), may hold values from -0.1875 to 0.1875
- w_key: bfloat16 [1024, 1024], P(None, 'head'), may hold values from -0.1875 to 0.1875
- w_value: bfloat16 [1024, 1024], P(None, 'head'), may hold values from -0.1875 to 0.1875
- w_gate: bfloat16 [1024, 1024], P(None, 'head'), may hold values from -0.1875 to 0.1875
- w_out: bfloat16 [1024, 1024], P('head'), may hold values from -0.1875 to 0.1875
- f_value: bfloat16 [1024, 2816], P('dp', 'head'), may hold values from -0.1875 to 0.1875
- f_gate: bfloat16 [1024, 2816], P('dp', 'head'), may hold values from -0.1875 to 0.1875
- f_out: bfloat16 [2816, 1024], P('head', 'dp'), may hold values from -0.109375 to 0.109375
- cotangent: bfloat16 [16384, 1024], P(('dp', 'head')), may hold values from -6 to 6
Outputs:
- output: bfloat16 [16384, 1024], P(('dp', 'head'))
- d_tokens: float32 [16384, 1024], P(('dp', 'head'))
- d_w_query: float32 [1024, 1024], P(None, 'head')
- d_w_key: float32 [1024, 1024], P(None, 'head')
- d_w_value: float32 [1024, 1024], P(None, 'head')
- d_w_gate: float32 [1024, 1024], P(None, 'head')
- d_w_out: float32 [1024, 1024], P('head')
- d_f_value: float32 [1024, 2816], P('dp', 'head')
- d_f_gate: float32 [1024, 2816], P('dp', 'head')
- d_f_out: float32 [2816, 1024], P('head', 'dp')
Inputs may be any that keep to these rules, and one draw needn't show every extreme that they name: `lengths`: each bucket holds a single slot, and that slot's sequence has length 1024.
All inputs are finite; a program needn't handle non-finite values.
Results may differ from a plain program's by a relative error of at most 0.022.
Values may be sent and summed in bfloat16 or wider, within the bound.
A program may use at most 192 MiB of HBM per device.

v0:
```python
import jax
import jax.numpy as jnp
from jax import lax
from jax.sharding import PartitionSpec as P

D = 1024
HD = 128
SEQ_DEV = 1
SLOT = 1024
BLOCK = 512
epsilon = 1e-06


def normalize(values):
    factor = lax.rsqrt(jnp.mean(values * values, axis=-1, keepdims=True) + epsilon)
    return (values * factor, factor)


def norm_back(grad_normed, normed, factor):
    inner_sum = jnp.mean(grad_normed * normed, axis=-1, keepdims=True)
    return factor * (grad_normed - normed * inner_sum)


def silu_slope(values):
    sigmoid = jax.nn.sigmoid(values)
    return sigmoid * (1.0 + values * (1.0 - sigmoid))


def matmul(left_side, right_side):
    return jnp.dot(left_side, right_side, preferred_element_type=jnp.float32)


def matmul_right_t(left_side, right_side):
    return lax.dot_general(
        left_side, right_side, (((1,), (1,)), ((), ())), preferred_element_type=jnp.float32
    )


def matmul_left_t(left_side, right_side):
    return lax.dot_general(
        left_side, right_side, (((0,), (0,)), ((), ())), preferred_element_type=jnp.float32
    )


def exact(form, left_side, right_side):
    return jnp.einsum(form, left_side, right_side, precision=lax.Precision.HIGHEST)


def decay_tables(rates):
    offsets = jnp.arange(BLOCK).astype(jnp.float32)
    spread = offsets[:, None] - offsets[None, :]
    causal = spread >= 0
    within = jnp.where(
        causal[None], jnp.exp(-rates[:, None, None] * jnp.where(causal, spread, 0.0)[None]), 0.0
    )
    first_decay = jnp.exp(-rates[:, None] * (offsets[None, :] + 1.0))
    last_decay = jnp.exp(-rates[:, None] * (BLOCK - 1.0 - offsets[None, :]))
    block_decay = jnp.exp(-rates * BLOCK)
    return (within, first_decay, last_decay, block_decay)


def to_blocks(values, heads):
    shaped = values.reshape(SEQ_DEV, SLOT // BLOCK, BLOCK, heads, HD)
    return shaped.transpose(1, 0, 3, 2, 4)


def from_blocks(blocks):
    return blocks.transpose(1, 0, 3, 2, 4).reshape(-1, blocks.shape[2] * blocks.shape[4])


def lightning_forward(query, keys, values, tables):
    within, first_decay, last_decay, block_decay = tables

    def advance(carried, inputs):
        query_blk, keys_blk, values_blk = inputs
        scores = jnp.einsum(
            "shbd,shcd->shbc", query_blk, keys_blk, preferred_element_type=jnp.float32
        )
        weights = (scores * within[None]).astype(jnp.bfloat16)
        inner_sum = jnp.einsum(
            "shbc,shcd->shbd", weights, values_blk, preferred_element_type=jnp.float32
        )
        outer_sum = first_decay[None, :, :, None] * exact(
            "shbd,shde->shbe", query_blk.astype(jnp.float32), carried
        )
        keys_scaled = keys_blk.astype(jnp.float32) * last_decay[None, :, :, None]
        update = exact("shbd,shbe->shde", keys_scaled, values_blk.astype(jnp.float32))
        return (
            block_decay[None, :, None, None] * carried + update,
            (inner_sum + outer_sum, carried),
        )

    initial = jnp.zeros((SEQ_DEV, query.shape[2], HD, HD), jnp.float32)
    final_state, (mixed, states) = lax.scan(advance, initial, (query, keys, values))
    return (mixed, states)


def lightning_backward(query, keys, values, grads, states, tables):
    within, first_decay, last_decay, block_decay = tables

    def retreat(later_grad, inputs):
        query_blk, keys_blk, values_blk, grad_blk, carried = inputs
        scores = jnp.einsum(
            "shbd,shcd->shbc", query_blk, keys_blk, preferred_element_type=jnp.float32
        )
        weights = (scores * within[None]).astype(jnp.bfloat16)
        d_weights = jnp.einsum(
            "shbd,shcd->shbc", grad_blk, values_blk, preferred_element_type=jnp.float32
        )
        d_scores = (d_weights * within[None]).astype(jnp.bfloat16)
        d_query = jnp.einsum(
            "shbc,shcd->shbd", d_scores, keys_blk, preferred_element_type=jnp.float32
        )
        d_keys = jnp.einsum(
            "shbc,shbd->shcd", d_scores, query_blk, preferred_element_type=jnp.float32
        )
        d_values = jnp.einsum(
            "shbc,shbd->shcd", weights, grad_blk, preferred_element_type=jnp.float32
        )
        grad_scaled = grad_blk.astype(jnp.float32) * first_decay[None, :, :, None]
        keys_scaled = keys_blk.astype(jnp.float32) * last_decay[None, :, :, None]
        d_query = d_query + exact("shbe,shde->shbd", grad_scaled, carried)
        d_keys = d_keys + last_decay[None, :, :, None] * exact(
            "shbe,shde->shbd", values_blk.astype(jnp.float32), later_grad
        )
        d_values = d_values + exact("shbd,shde->shbe", keys_scaled, later_grad)
        earlier = block_decay[None, :, None, None] * later_grad + exact(
            "shbd,shbe->shde", query_blk.astype(jnp.float32), grad_scaled
        )
        return (earlier, (d_query, d_keys, d_values))

    initial = jnp.zeros((SEQ_DEV, query.shape[2], HD, HD), jnp.float32)
    first_grad, results = lax.scan(
        retreat, initial, (query, keys, values, grads, states), reverse=True
    )
    return results


def body(
    tokens,
    lengths,
    decay,
    w_query,
    w_key,
    w_value,
    w_gate,
    w_out,
    f_value,
    f_gate,
    f_out,
    cotangent,
):
    own_rows = tokens.shape[0]
    first_row = lax.axis_index("head") * own_rows
    heads_here = decay.shape[0]
    tables = decay_tables(decay)
    positions = first_row + jnp.arange(own_rows, dtype=jnp.int32)
    slot_match = (positions // SLOT)[:, None] == jnp.arange(SEQ_DEV, dtype=jnp.int32)[None, :]
    length_of = jnp.sum(jnp.where(slot_match, lengths[None, :], 0), axis=1)
    keep_rows = (positions % SLOT < length_of).astype(jnp.float32)[:, None]
    inputs_f = tokens.astype(jnp.float32)
    normed, scale_in = normalize(inputs_f)
    gathered = lax.all_gather(normed.astype(jnp.bfloat16), "head", axis=0, tiled=True)
    query_pre = matmul(gathered, w_query)
    keys_pre = matmul(gathered, w_key)
    values_pre = matmul(gathered, w_value)
    gate_pre = matmul(gathered, w_gate)
    query_blocks = to_blocks(jax.nn.silu(query_pre).astype(jnp.bfloat16), heads_here)
    keys_blocks = to_blocks(jax.nn.silu(keys_pre).astype(jnp.bfloat16), heads_here)
    values_blocks = to_blocks(values_pre.astype(jnp.bfloat16), heads_here)
    mixed_blocks, states = lightning_forward(query_blocks, keys_blocks, values_blocks, tables)
    mixed = from_blocks(mixed_blocks)
    squares = lax.psum(jnp.sum(mixed * mixed, axis=1), "head")
    scale_out = lax.rsqrt(squares / D + epsilon)[:, None]
    mixed_unit = mixed * scale_out
    gated = (mixed_unit * gate_pre).astype(jnp.bfloat16)
    branch = lax.psum_scatter(
        matmul(gated, w_out).astype(jnp.bfloat16), "head", scatter_dimension=0, tiled=True
    ).astype(jnp.float32)
    middle = inputs_f + branch
    mid_normed, scale_mid = normalize(middle)
    mid_all = lax.all_gather(mid_normed.astype(jnp.bfloat16), "head", axis=0, tiled=True)
    value_full, gate_full = (
        lax.all_gather(f_value, "dp", axis=0, tiled=True),
        lax.all_gather(f_gate, "dp", axis=0, tiled=True),
    )
    down_full = lax.all_gather(f_out, "dp", axis=1, tiled=True)
    value_ffn = matmul(mid_all, value_full)
    gate_ffn = matmul(mid_all, gate_full)
    hidden = (value_ffn * gate_ffn).astype(jnp.bfloat16)
    ffn_branch = lax.psum_scatter(
        matmul(hidden, down_full).astype(jnp.bfloat16), "head", scatter_dimension=0, tiled=True
    ).astype(jnp.float32)
    output = ((middle + ffn_branch) * keep_rows).astype(jnp.bfloat16)
    grad_out = cotangent.astype(jnp.float32) * keep_rows
    grad_all = lax.all_gather(grad_out.astype(jnp.bfloat16), "head", axis=0, tiled=True)
    grad_hidden = matmul_right_t(grad_all, down_full)
    d_value_ffn = (grad_hidden * gate_ffn).astype(jnp.bfloat16)
    d_gate_ffn = (grad_hidden * value_ffn).astype(jnp.bfloat16)
    d_mid_normed = lax.psum_scatter(
        (matmul_right_t(d_value_ffn, value_full) + matmul_right_t(d_gate_ffn, gate_full)).astype(
            jnp.bfloat16
        ),
        "head",
        scatter_dimension=0,
        tiled=True,
    ).astype(jnp.float32)
    grad_middle = grad_out + norm_back(d_mid_normed, mid_normed, scale_mid)
    joined = jnp.concatenate([d_value_ffn, d_gate_ffn], axis=1)
    hidden_here = hidden.shape[1]
    shares = lax.psum_scatter(
        jnp.concatenate(
            [matmul_left_t(mid_all, joined), matmul_left_t(grad_all, hidden)], axis=1
        ).astype(jnp.bfloat16),
        "dp",
        scatter_dimension=0,
        tiled=True,
    ).astype(jnp.float32)
    d_f_value = shares[:, :hidden_here]
    d_f_gate = shares[:, hidden_here : 2 * hidden_here]
    d_f_out = shares[:, 2 * hidden_here :].T
    grad_rows = lax.all_gather(grad_middle.astype(jnp.bfloat16), "head", axis=0, tiled=True)
    d_gated = matmul_right_t(grad_rows, w_out)
    d_w_out_local = matmul_left_t(gated, grad_rows)
    d_gate_pre = (d_gated * mixed_unit).astype(jnp.bfloat16)
    d_unit = d_gated * gate_pre
    inner_out = lax.psum(jnp.sum(d_unit * mixed_unit, axis=1), "head")
    d_mixed = (scale_out * (d_unit - mixed_unit * (inner_out / D)[:, None])).astype(jnp.bfloat16)
    d_query, d_keys, d_values = lightning_backward(
        query_blocks, keys_blocks, values_blocks, to_blocks(d_mixed, heads_here), states, tables
    )
    d_query_pre = (from_blocks(d_query) * silu_slope(query_pre)).astype(jnp.bfloat16)
    d_keys_pre = (from_blocks(d_keys) * silu_slope(keys_pre)).astype(jnp.bfloat16)
    d_values_pre = from_blocks(d_values).astype(jnp.bfloat16)
    total = matmul_right_t(d_query_pre, w_query) + matmul_right_t(d_keys_pre, w_key)
    d_normed = lax.psum_scatter(
        (total + matmul_right_t(d_values_pre, w_value) + matmul_right_t(d_gate_pre, w_gate)).astype(
            jnp.bfloat16
        ),
        "head",
        scatter_dimension=0,
        tiled=True,
    ).astype(jnp.float32)
    d_tokens = grad_middle + norm_back(d_normed, normed, scale_in)
    grads_attention = (
        lax.psum(matmul_left_t(gathered, d_query_pre).astype(jnp.bfloat16), "dp").astype(
            jnp.float32
        ),
        lax.psum(matmul_left_t(gathered, d_keys_pre).astype(jnp.bfloat16), "dp").astype(
            jnp.float32
        ),
        lax.psum(matmul_left_t(gathered, d_values_pre).astype(jnp.bfloat16), "dp").astype(
            jnp.float32
        ),
        lax.psum(matmul_left_t(gathered, d_gate_pre).astype(jnp.bfloat16), "dp").astype(
            jnp.float32
        ),
        lax.psum(d_w_out_local.astype(jnp.bfloat16), "dp").astype(jnp.float32),
    )
    return (
        output,
        d_tokens,
        grads_attention[0],
        grads_attention[1],
        grads_attention[2],
        grads_attention[3],
        grads_attention[4],
        d_f_value,
        d_f_gate,
        d_f_out,
    )


def solution(mesh):
    placed = (
        P(("dp", "head"), None),
        P("dp"),
        P("head"),
        P(None, "head"),
        P(None, "head"),
        P(None, "head"),
        P(None, "head"),
        P("head", None),
        P("dp", "head"),
        P("dp", "head"),
        P("head", "dp"),
        P(("dp", "head"), None),
    )
    return jax.shard_map(
        body,
        mesh=mesh,
        in_specs=placed,
        out_specs=(
            P(("dp", "head"), None),
            P(("dp", "head"), None),
            P(None, "head"),
            P(None, "head"),
            P(None, "head"),
            P(None, "head"),
            P("head", None),
            P("dp", "head"),
            P("dp", "head"),
            P("head", "dp"),
        ),
        check_vma=False,
    )
```

profile of v0, /device:TPU:0, one launch (start us, length us, event | category | flops | bytes accessed | tf_op | source)
XLA Modules:
  0.0 686.0 jit_solution(16797415050043910649)
XLA Ops:
  15.0 33.8 %all-gather.8.cloned.1.call-done = bf16[1024,1024]{1,0:T(8,128)(2,1)} async-done(((bf16[512,1024]{1,0:T(8,128)(2,1)}), bf16[1024,1024]{1,0:T(8,128)(2,1)}) %all-gather.8.cloned.1.call-update) | async-done | bytes 2097168 | tf_op jit(solution)/shard_map/all_gather | solution.py:163
  48.8 4.4 multiply_convert_fusion.8
  69.1 15.1 %while.40 = (s32[]{:T(128)}, f32[1,4,128,128]{3,2,1,0:T(8,128)S(1)}, f32[2,1,4,512,128]{4,3,2,1,0:T(8,128)}, f32[2,1,4,128,128]{4,3,2,1,0:T(8,128)}, f32[4]{0:T(...) while((s32[]{:T(128)}, ...), condition=%wide.region_2.3_spmd.clone.clone.clone, body=%wide.region_1.2_spmd.clone.clone.clone.sunk | while | flops 1347751936 | bytes 17343232 | solution.py:94
  86.4 4.1 copy.42
  92.6 5.1 psum.49
  97.7 4.5 multiply_convert_fusion.6
  106.5 31.3 %reduce-scatter.6.cloned.1.call-done = bf16[512,1024]{1,0:T(8,128)(2,1)} async-done(((bf16[1024,1024]{1,0:T(8,128)(2,1)}), bf16[512,1024]{1,0:T(8,128)(2,1)}) %reduce-scatter.6.cloned.1.call-update) | async-done | bytes 1048592 | tf_op jit(solution)/shard_map/reduce_scatter | solution.py:177
  145.4 7.4 %all-gather.12.cloned.1.call-done = bf16[1024,1408]{1,0:T(8,128)(2,1)} async-done(((bf16[64,1408]{1,0:T(8,128)(2,1)}), bf16[1024,1408]{1,0:T(8,128)(2,1)}) %all-gather.12.cloned.1.call-update) | async-done | bytes 2883600 | tf_op jit(solution)/shard_map/all_gather | solution.py:184
  152.9 33.7 %all-gather.10.cloned.1.call-done = bf16[1024,1024]{1,0:T(8,128)(2,1)} async-done(((bf16[512,1024]{1,0:T(8,128)(2,1)}), bf16[1024,1024]{1,0:T(8,128)(2,1)}) %all-gather.10.cloned.1.call-update) | async-done | bytes 2097168 | tf_op jit(solution)/shard_map/all_gather | solution.py:182
  186.6 8.3 %fusion.155 = f32[1024,1408]{1,0:T(8,128)} fusion(bf16[1024,1024]{1,0:T(8,128)(2,1)} %all-gather.10.cloned.1.call-done, bf16[1024,1408]{1,0:T(8,128)(2,1)} %all-gather.12.cloned.1.call-done), kind=kOutput, calls=%fused_computation.209 | convolution fusion | flops 2952790016 | bytes 10747904 | tf_op jit(solution)/shard_map/dot_general | solution.py:30
  194.9 38.1 %all-gather.14.cloned.1.call-done = bf16[1024,1408]{1,0:T(8,128)(2,1)} async-done(((bf16[64,1408]{1,0:T(8,128)(2,1)}), bf16[1024,1408]{1,0:T(8,128)(2,1)}) %all-gather.14.cloned.1.call-update) | async-done | bytes 2883600 | tf_op jit(solution)/shard_map/all_gather | solution.py:185
  233.0 8.4 %fusion.156 = f32[1024,1408]{1,0:T(8,128)} fusion(bf16[1024,1024]{1,0:T(8,128)(2,1)} %all-gather.10.cloned.1.call-done, bf16[1024,1408]{1,0:T(8,128)(2,1)} %all-gather.14.cloned.1.call-done), kind=kOutput, calls=%fused_computation.210 | convolution fusion | flops 2952790016 | bytes 10747904 | tf_op jit(solution)/shard_map/dot_general | solution.py:30
  241.4 25.5 %all-gather.18.cloned.1.call-done = bf16[1024,1024]{1,0:T(8,128)(2,1)} async-done(((bf16[512,1024]{1,0:T(8,128)(2,1)}), bf16[1024,1024]{1,0:T(8,128)(2,1)}) %all-gather.18.cloned.1.call-update) | async-done | bytes 2097168 | tf_op jit(solution)/shard_map/all_gather | solution.py:196
  266.8 46.6 %all-gather.16.cloned.1.call-done = bf16[1408,1024]{0,1:T(8,128)(2,1)} async-done(((bf16[1408,64]{0,1:T(8,128)(2,1)}), bf16[1408,1024]{0,1:T(8,128)(2,1)}) %all-gather.16.cloned.1.call-update) | async-done | bytes 2883600 | tf_op jit(solution)/shard_map/all_gather | solution.py:187
  313.4 11.0 %multiply_convert_fusion = (bf16[1024,1408]{1,0:T(8,128)(2,1)S(1)}, bf16[1024,1408]{1,0:T(8,128)(2,1)}, bf16[1024,1408]{1,0:T(8,128)(2,1)S(1)}) fusion(f32[1024,1408]{1,0:T(8,128)} %fusion.155, f32[1024,1408]{1,0:T(8,128)} %fusion.156, bf16[1024,1024]{1,0:T(8,128)(2,1)} %all-gather.18.cloned.1.call-done, bf16[1408,1024]{0,1:T(8,128)(2,1)} %all-gather.16.cloned.1.call-done), kind=kOutput, calls=%fused_computation.120 | convolution fusion | flops 2961440768 | bytes 25165824 | tf_op jit(solution)/shard_map/dot_general | solution.py:34
  324.4 3.4 fusion.157
  328.3 4.6 add_convert_fusion.1
  333.0 30.6 %reduce-scatter.10.cloned.1.call-done = bf16[512,1024]{1,0:T(8,128)(2,1)} async-done(((bf16[1024,1024]{1,0:T(8,128)(2,1)}), bf16[512,1024]{1,0:T(8,128)(2,1)}) %reduce-scatter.10.cloned.1.call-update) | async-done | bytes 1048592 | tf_op jit(solution)/shard_map/reduce_scatter | solution.py:200
  371.5 29.3 %all-gather.20.cloned.1.call-done = bf16[1024,1024]{1,0:T(8,128)(2,1)} async-done(((bf16[512,1024]{1,0:T(8,128)(2,1)}), bf16[1024,1024]{1,0:T(8,128)(2,1)}) %all-gather.20.cloned.1.call-update) | async-done | bytes 2097168 | tf_op jit(solution)/shard_map/all_gather | solution.py:222
  400.8 5.3 multiply_reduce_fusion
  406.1 4.9 psum.50
  418.9 36.7 %while.41 = (s32[]{:T(128)}, f32[1,4,128,128]{3,2,1,0:T(8,128)S(1)}, f32[2,1,4,512,128]{4,3,2,1,0:T(8,128)}, f32[2,1,4,512,128]{4,3,2,1,0:T(8,128)}, bf16[2,1,4,...) while((s32[]{:T(128)}, ...), condition=%wide.region_13.14_spmd.clone.clone.clone, body=%wide.region_12.13_spmd.clone.clone.clone.sunk | while | flops 2964131840 | bytes 44889964 | solution.py:133
  426.5 3.3 fusion.266
  429.9 3.3 fusion.269
  444.8 3.3 fusion.266
  486.5 7.5 %convolution_convert_fusion.1 = bf16[1024,1024]{1,0:T(8,128)(2,1)} fusion(bf16[1024,1408]{1,0:T(8,128)(2,1)} %get-tuple-element.714, bf16[1408,1024]{0,1:T(8,128)(2,1)} %all-gather.16.cloned.1.call-done), kind=kOutput, calls=%fused_computation.160 | convolution fusion | flops 2953838592 | bytes 7864320 | tf_op jit(solution)/shard_map/dot_general | solution.py:30
  495.7 5.7 convolution_convert_fusion
  501.4 6.8 fusion.121
  508.3 3.8 pad_maximum_fusion
  512.1 115.8 %all-reduce.3.cloned.1.call-done = (bf16[1024,512]{1,0:T(8,128)(2,1)}, bf16[1024,512]{1,0:T(8,128)(2,1)}, bf16[1024,512]{1,0:T(8,128)(2,1)}, bf16[1024,512]{1,0:T(8,128)(2,1)}, bf16[512,1024]{1,0:T(8,128)(2,1)}) async-done(((bf16[1024,512]{1,0:T(8,128)(2,1)}, bf16[1024,512]{1,0:T(8,128)(2,1)}, bf16[1024,512]{1,0:T(8,128)(2,1)}, bf16[1024,512]{1,0:T(8,128)(2,1)}, bf16[512,1024]{1,0:T(8,128)(2,1)}), ...) | async-done | bytes 5242896 | tf_op jit(solution)/shard_map/psum | solution.py:246
  639.0 4.5 fusion.131
  643.4 31.9 %reduce-scatter.14.cloned.1.call-done = bf16[64,4224]{1,0:T(8,128)(2,1)} async-done(((bf16[1024,4224]{1,0:T(8,128)(2,1)}), bf16[64,4224]{1,0:T(8,128)(2,1)}) %reduce-scatter.14.cloned.1.call-update) | async-done | bytes 540688 | tf_op jit(solution)/shard_map/reduce_scatter | solution.py:211
  (238 shorter events, 142.1 us)
Async XLA Ops:
  8.0 95.2 %copy-start = (bf16[512,1024]{1,0:T(8,128)(2,1)S(1)}, bf16[512,1024]{1,0:T(8,128)(2,1)}, u32[]{:S(2)}) copy-start(bf16[512,1024]{1,0:T(8,128)(2,1)} %param.23) | copy-start | bytes 3145732
  8.0 40.8 %all-gather.8.cloned.1.call-start = ((), (), s32[]{:S(2)}) async-start(), calls=%async_computation.5 | async-start | bytes 3145728 | tf_op jit(solution)/shard_map/all_gather | solution.py:163
  8.1 4.8 copy-start.51
  10.3 38.5 %copy-start.48 = (bf16[1024,512]{1,0:T(8,128)(2,1)S(1)}, bf16[1024,512]{1,0:T(8,128)(2,1)}, u32[]{:S(2)}) copy-start(bf16[1024,512]{1,0:T(8,128)(2,1)} %param.20) | copy-start | bytes 3145732
  12.8 125.0 %reduce-scatter.6.cloned.1.call-start = ((), (), s32[]{:S(2)}) async-start(), calls=%async_computation.6 | async-start | bytes 3145728 | tf_op jit(solution)/shard_map/reduce_scatter | solution.py:177
  72.1 3.7 copy-start.13
  79.7 3.7 copy-start.13
  84.2 6.3 copy-start.6
  92.5 9.6 %copy-start.4 = (f32[64,8,2,512]{3,1,2,0:T(8,128)}, f32[64,8,2,512]{3,1,2,0:T(8,128)S(1)}, u32[]{:S(2)}) copy-start(f32[64,8,2,512]{3,1,2,0:T(8,128)S(1)} %copy.52) | copy-start | bytes 6291460
  105.8 32.0 %copy-start.2 = (bf16[512,1024]{1,0:T(8,128)(2,1)S(1)}, bf16[512,1024]{1,0:T(8,128)(2,1)}, u32[]{:S(2)}) copy-start(bf16[512,1024]{1,0:T(8,128)(2,1)} %param.16) | copy-start | bytes 3145732
  105.8 47.0 %all-gather.12.cloned.1.call-start = ((), (), s32[]{:S(2)}) async-start(), calls=%async_computation.8 | async-start | bytes 3063808 | tf_op jit(solution)/shard_map/all_gather | solution.py:184
  106.4 80.2 %all-gather.10.cloned.1.call-start = ((), (), s32[]{:S(2)}) async-start(), calls=%async_computation.7 | async-start | bytes 3145728 | tf_op jit(solution)/shard_map/all_gather | solution.py:182
  140.8 92.1 %all-gather.14.cloned.1.call-start = ((), (), s32[]{:S(2)}) async-start(), calls=%async_computation.9 | async-start | bytes 3063808 | tf_op jit(solution)/shard_map/all_gather | solution.py:185
  141.4 125.4 %all-gather.18.cloned.1.call-start = ((), (), s32[]{:S(2)}) async-start(), calls=%async_computation.12 | async-start | bytes 3145728 | tf_op jit(solution)/shard_map/all_gather | solution.py:196
  144.6 168.8 %all-gather.16.cloned.1.call-start = ((), (), s32[]{:S(2)}) async-start(), calls=%async_computation.10 | async-start | bytes 3063808 | tf_op jit(solution)/shard_map/all_gather | solution.py:187
  145.4 218.3 %reduce-scatter.10.cloned.1.call-start = ((), (), s32[]{:S(2)}) async-start(), calls=%async_computation.13 | async-start | bytes 3145728 | tf_op jit(solution)/shard_map/reduce_scatter | solution.py:200
  313.4 11.0 %copy-start.44 = (bf16[1024,1408]{1,0:T(8,128)(2,1)S(1)}, bf16[1024,1408]{1,0:T(8,128)(2,1)}, u32[]{:S(2)}) copy-start(bf16[1024,1408]{1,0:T(8,128)(2,1)} %all-gather.12.cloned.1.call-done) | copy-start | bytes 8650756
  324.4 3.9 copy-start.45
  333.0 67.8 %all-gather.20.cloned.1.call-start = ((), (), s32[]{:S(2)}) async-start(), calls=%async_computation.14 | async-start | bytes 3145728 | tf_op jit(solution)/shard_map/all_gather | solution.py:222
  367.5 33.3 %copy-start.5 = (f32[64,8,2,512]{3,1,2,0:T(8,128)S(1)}, f32[64,8,2,512]{3,1,2,0:T(8,128)}, u32[]{:S(2)}) copy-start(f32[64,8,2,512]{3,1,2,0:T(8,128)} %copy-done.4) | copy-start | bytes 6291460
  367.5 260.3 %all-reduce.3.cloned.1.call-start = ((), (), s32[]{:S(2)}) async-start(), calls=%async_computation.17 | async-start | bytes 10485760 | tf_op jit(solution)/shard_map/psum | solution.py:246
  426.2 3.7 copy-start.8
  426.2 3.7 copy-start.10
  444.5 3.7 copy-start.8
  462.4 11.0 %copy-start.38 = (bf16[1,2,512,4,128]{4,3,2,1,0:T(4,128)(2,1)}, bf16[1,2,512,4,128]{4,3,2,1,0:T(4,128)(2,1)S(1)}, u32[]{:S(2)}) copy-start(bf16[1,2,512,4,128]{4,3,2,1,0:T(4,128)(2,1)S(1)} %copy.46) | copy-start | bytes 3145732
  478.0 159.2 %reduce-scatter.12.cloned.1.call-start = ((), (), s32[]{:S(2)}) async-start(), calls=%async_computation.15 | async-start | bytes 3145728 | tf_op jit(solution)/shard_map/reduce_scatter | solution.py:236
  486.5 152.5 %reduce-scatter.8.cloned.1.call-start = ((), (), s32[]{:S(2)}) async-start(), calls=%async_computation.11 | async-start | bytes 3145728 | tf_op jit(solution)/shard_map/reduce_scatter | solution.py:191
  494.1 181.3 %reduce-scatter.14.cloned.1.call-start = ((), (), s32[]{:S(2)}) async-start(), calls=%async_computation.16 | async-start | bytes 9191424 | tf_op jit(solution)/shard_map/reduce_scatter | solution.py:211
  495.7 5.7 copy-start.26
  495.7 5.7 copy-start.28
  495.7 5.7 copy-start.46
  639.0 39.3 %copy-start.1 = (bf16[512,1024]{1,0:T(8,128)(2,1)S(1)}, bf16[512,1024]{1,0:T(8,128)(2,1)}, u32[]{:S(2)}) copy-start(bf16[512,1024]{1,0:T(8,128)(2,1)} %param.23) | copy-start | bytes 3145732
  (41 other events, 85.5 us)
Sparse Core Ops, SparseCore 0:
  12.9 35.8 all-gather.7
  106.0 31.7 reduce-scatter.5
  333.1 30.4 reduce-scatter.9
  367.6 33.1 all-gather.19
  486.6 31.8 reduce-scatter.11
  520.7 31.8 reduce-scatter.7
  557.2 118.1 reduce-scatter.13
Sparse Core Ops, SparseCore 1:
  108.9 43.9 all-gather.11
  154.9 31.6 all-gather.9
  189.0 43.9 all-gather.13
  235.2 31.6 all-gather.17
  269.4 43.9 all-gather.15
  478.1 149.7 all-reduce.2
where the time goes:
time: 694 us; the launch traced here: 686 us
  waiting for transfers between devices  426 us (61%)
  matrix products  147 us (21%)
  other arithmetic  43.4 us (6%)
  local copies, waits for them, and re-layouts  41 us (6%)
  between operations  17.1 us (2%)
  blocking collectives  10 us (1%)
    psum x1, waiting for transfers between devices, body(): lax.psum(matmul_left_t(gathered, d_query_pre).astype(jnp.bfloat16), 'dp')  116 us
    all_gather x1, waiting for transfers between devices, body(): down_full = lax.all_gather(f_out, 'dp', axis=1, tiled=True)  46.6 us
    dot_general x8, matrix products, matmul(): return jnp.dot(left_side, right_side, preferred_element_type=jnp.float32)  41.9 us
    all_gather x1, waiting for transfers between devices, body(): lax.all_gather(f_gate, 'dp', axis=0, tiled=True)  38.1 us
    all_gather x1, waiting for transfers between devices, body(): lax.all_gather(normed.astype(jnp.bfloat16), 'head', axis=0, tiled=True)  33.8 us
    all_gather x1, waiting for transfers between devices, body(): lax.all_gather(mid_normed.astype(jnp.bfloat16), 'head', axis=0, tiled=True)  33.7 us
    dot_general x8, matrix products, matmul_right_t(): lax.dot_general(left_side, right_side, (((1,), (1,)), ((), ())), preferre...  32.3 us
    reduce_scatter x1, waiting for transfers between devices, body(): lax.psum_scatter(jnp.concatenate([matmul_left_t(mid_all, joined), matmul_...  31.9 us
  transfers between devices with their start and end apart: 13, of which 11 were waited for; matrix products, arithmetic and copies ran while one was open for 11% of the time, Pallas kernels for 0%

commit v1 on v0

--- a/solution.py
+++ b/solution.py
@@ -243,9 +243,9 @@
     ).astype(jnp.float32)
     d_tokens = grad_middle + norm_back(d_normed, normed, scale_in)
     grads_attention = (
-        lax.psum(matmul_left_t(gathered, d_query_pre).astype(jnp.bfloat16), "dp").astype(
-            jnp.float32
-        ),
+        jnp.sum(
+            lax.all_gather(matmul_left_t(gathered, d_query_pre).astype(jnp.bfloat16), "dp"), axis=0
+        ).astype(jnp.float32),
         lax.psum(matmul_left_t(gathered, d_keys_pre).astype(jnp.bfloat16), "dp").astype(
             jnp.float32
         ),

time: 694 us -> 784 us (1.13)
  waiting for transfers between devices: 426 us -> 504 us
  other arithmetic: 43.4 us -> 52.4 us
    reduce_scatter x1, waiting for transfers between devices: 31.9 us -> 156 us  [body(): lax.psum_scatter(jnp.concatenate([matmul_left_t(mid_all, joined), matmul_...]
    psum x1, waiting for transfers between devices: 116 us -> 68.9 us  [body(): lax.psum(matmul_left_t(gathered, d_keys_pre).astype(jnp.bfloat16), 'dp')]
    reduce_sum x0 -> x1, other arithmetic: none -> 8.99 us  [body(): jnp.sum(lax.all_gather(matmul_left_t(gathered, d_query_pre).astype(jnp.bf...]
  transfers between devices with their start and end apart: 13 -> 14, of which waited for: 11 -> 11; matrix products, arithmetic and copies ran while one was open for 11% -> 11% of each run, Pallas kernels for 0% -> 0%
where the time goes in v1:
time: 784 us; the launch traced here: 775 us
  waiting for transfers between devices  504 us (64%)
  matrix products  147 us (19%)
  other arithmetic  52.4 us (7%)
  local copies, waits for them, and re-layouts  43.5 us (6%)
  between operations  17 us (2%)
  blocking collectives  10 us (1%)
    reduce_scatter x1, waiting for transfers between devices, body(): lax.psum_scatter(jnp.concatenate([matmul_left_t(mid_all, joined), matmul_...  156 us
    psum x1, waiting for transfers between devices, body(): lax.psum(matmul_left_t(gathered, d_keys_pre).astype(jnp.bfloat16), 'dp')  68.9 us
    all_gather x1, waiting for transfers between devices, body(): down_full = lax.all_gather(f_out, 'dp', axis=1, tiled=True)  46.6 us
    dot_general x8, matrix products, matmul(): return jnp.dot(left_side, right_side, preferred_element_type=jnp.float32)  41.9 us
    all_gather x1, waiting for transfers between devices, body(): lax.all_gather(f_gate, 'dp', axis=0, tiled=True)  38.1 us
    all_gather x1, waiting for transfers between devices, body(): lax.all_gather(normed.astype(jnp.bfloat16), 'head', axis=0, tiled=True)  33.7 us
    all_gather x1, waiting for transfers between devices, body(): lax.all_gather(mid_normed.astype(jnp.bfloat16), 'head', axis=0, tiled=True)  33.7 us
    dot_general x8, matrix products, matmul_right_t(): lax.dot_general(left_side, right_side, (((1,), (1,)), ((), ())), preferre...  32.3 us
  transfers between devices with their start and end apart: 14, of which 11 were waited for; matrix products, arithmetic and copies ran while one was open for 11% of the time, Pallas kernels for 0%

profile of v1, /device:TPU:0, one launch (start us, length us, event | category | flops | bytes accessed | tf_op | source)
XLA Modules:
  0.0 775.3 jit_solution(12640202401142251131)
XLA Ops:
  15.0 33.7 %all-gather.10.cloned.1.call-done = bf16[1024,1024]{1,0:T(8,128)(2,1)} async-done(((bf16[512,1024]{1,0:T(8,128)(2,1)}), bf16[1024,1024]{1,0:T(8,128)(2,1)}) %all-gather.10.cloned.1.call-update) | async-done | bytes 2097168 | tf_op jit(solution)/shard_map/all_gather | solution.py:163
  48.8 4.4 multiply_convert_fusion.8
  69.1 15.1 %while.40 = (s32[]{:T(128)}, f32[1,4,128,128]{3,2,1,0:T(8,128)S(1)}, f32[2,1,4,512,128]{4,3,2,1,0:T(8,128)}, f32[2,1,4,128,128]{4,3,2,1,0:T(8,128)}, f32[4]{0:T(...) while((s32[]{:T(128)}, ...), condition=%wide.region_2.3_spmd.clone.clone.clone, body=%wide.region_1.2_spmd.clone.clone.clone.sunk | while | flops 1347751936 | bytes 17343232 | solution.py:94
  86.4 4.1 copy.42
  92.6 5.1 psum.42
  97.7 4.5 multiply_convert_fusion.6
  106.4 31.3 %reduce-scatter.6.cloned.1.call-done = bf16[512,1024]{1,0:T(8,128)(2,1)} async-done(((bf16[1024,1024]{1,0:T(8,128)(2,1)}), bf16[512,1024]{1,0:T(8,128)(2,1)}) %reduce-scatter.6.cloned.1.call-update) | async-done | bytes 1048592 | tf_op jit(solution)/shard_map/reduce_scatter | solution.py:177
  145.4 7.4 all-gather.14.cloned.1.call-done
  152.8 33.7 %all-gather.12.cloned.1.call-done = bf16[1024,1024]{1,0:T(8,128)(2,1)} async-done(((bf16[512,1024]{1,0:T(8,128)(2,1)}), bf16[1024,1024]{1,0:T(8,128)(2,1)}) %all-gather.12.cloned.1.call-update) | async-done | bytes 2097168 | tf_op jit(solution)/shard_map/all_gather | solution.py:182
  186.5 8.3 %fusion.155 = f32[1024,1408]{1,0:T(8,128)} fusion(bf16[1024,1024]{1,0:T(8,128)(2,1)} %all-gather.12.cloned.1.call-done, bf16[1024,1408]{1,0:T(8,128)(2,1)} %all-gather.14.cloned.1.call-done), kind=kOutput, calls=%fused_computation.209 | convolution fusion | flops 2952790016 | bytes 10747904 | tf_op jit(solution)/shard_map/dot_general | solution.py:30
  194.9 38.1 %all-gather.16.cloned.1.call-done = bf16[1024,1408]{1,0:T(8,128)(2,1)} async-done(((bf16[64,1408]{1,0:T(8,128)(2,1)}), bf16[1024,1408]{1,0:T(8,128)(2,1)}) %all-gather.16.cloned.1.call-update) | async-done | bytes 2883600 | tf_op jit(solution)/shard_map/all_gather | solution.py:185
  233.0 8.4 %fusion.156 = f32[1024,1408]{1,0:T(8,128)} fusion(bf16[1024,1024]{1,0:T(8,128)(2,1)} %all-gather.12.cloned.1.call-done, bf16[1024,1408]{1,0:T(8,128)(2,1)} %all-gather.16.cloned.1.call-done), kind=kOutput, calls=%fused_computation.210 | convolution fusion | flops 2952790016 | bytes 10747904 | tf_op jit(solution)/shard_map/dot_general | solution.py:30
  241.4 25.5 %all-gather.20.cloned.1.call-done = bf16[1024,1024]{1,0:T(8,128)(2,1)} async-done(((bf16[512,1024]{1,0:T(8,128)(2,1)}), bf16[1024,1024]{1,0:T(8,128)(2,1)}) %all-gather.20.cloned.1.call-update) | async-done | bytes 2097168 | tf_op jit(solution)/shard_map/all_gather | solution.py:196
  266.8 46.6 %all-gather.18.cloned.1.call-done = bf16[1408,1024]{0,1:T(8,128)(2,1)} async-done(((bf16[1408,64]{0,1:T(8,128)(2,1)}), bf16[1408,1024]{0,1:T(8,128)(2,1)}) %all-gather.18.cloned.1.call-update) | async-done | bytes 2883600 | tf_op jit(solution)/shard_map/all_gather | solution.py:187
  313.4 11.0 %multiply_convert_fusion = (bf16[1024,1408]{1,0:T(8,128)(2,1)S(1)}, bf16[1024,1408]{1,0:T(8,128)(2,1)}, bf16[1024,1408]{1,0:T(8,128)(2,1)S(1)}) fusion(f32[1024,1408]{1,0:T(8,128)} %fusion.155, f32[1024,1408]{1,0:T(8,128)} %fusion.156, bf16[1024,1024]{1,0:T(8,128)(2,1)} %all-gather.20.cloned.1.call-done, bf16[1408,1024]{0,1:T(8,128)(2,1)} %all-gather.18.cloned.1.call-done), kind=kOutput, calls=%fused_computation.120 | convolution fusion | flops 2961440768 | bytes 25165824 | tf_op jit(solution)/shard_map/dot_general | solution.py:34
  324.4 3.4 fusion.157
  328.3 4.6 add_convert_fusion.1
  333.0 30.6 %reduce-scatter.10.cloned.1.call-done = bf16[512,1024]{1,0:T(8,128)(2,1)} async-done(((bf16[1024,1024]{1,0:T(8,128)(2,1)}), bf16[512,1024]{1,0:T(8,128)(2,1)}) %reduce-scatter.10.cloned.1.call-update) | async-done | bytes 1048592 | tf_op jit(solution)/shard_map/reduce_scatter | solution.py:200
  371.3 29.5 %all-gather.22.cloned.1.call-done = bf16[1024,1024]{1,0:T(8,128)(2,1)} async-done(((bf16[512,1024]{1,0:T(8,128)(2,1)}), bf16[1024,1024]{1,0:T(8,128)(2,1)}) %all-gather.22.cloned.1.call-update) | async-done | bytes 2097168 | tf_op jit(solution)/shard_map/all_gather | solution.py:222
  400.8 5.4 multiply_reduce_fusion
  406.2 4.9 psum.43
  419.0 36.9 %while.41 = (s32[]{:T(128)}, f32[1,4,128,128]{3,2,1,0:T(8,128)S(1)}, f32[2,1,4,512,128]{4,3,2,1,0:T(8,128)}, f32[2,1,4,512,128]{4,3,2,1,0:T(8,128)}, bf16[2,1,4,...) while((s32[]{:T(128)}, ...), condition=%wide.region_13.14_spmd.clone.clone.clone, body=%wide.region_12.13_spmd.clone.clone.clone.sunk | while | flops 2964131840 | bytes 44889964 | solution.py:133
  426.6 3.3 fusion.266
  444.9 3.3 fusion.266
  484.8 7.5 convolution_convert_fusion.1
  494.0 5.7 convolution_convert_fusion
  499.7 6.8 fusion.121
  506.6 3.8 pad_maximum_fusion
  514.6 68.9 %all-reduce.3.cloned.1.call-done = (bf16[1024,512]{1,0:T(8,128)(2,1)}, bf16[1024,512]{1,0:T(8,128)(2,1)}, bf16[1024,512]{1,0:T(8,128)(2,1)}, bf16[512,1024]{1,0:T(8,128)(2,1)}) async-done(((bf16[1024,512]{1,0:T(8,128)(2,1)}, bf16[1024,512]{1,0:T(8,128)(2,1)}, bf16[1024,512]{1,0:T(8,128)(2,1)}, bf16[512,1024]{1,0:T(8,128)(2,1)}), (bf16[1024,512]{1,0:T(8,128)(2,1)}, bf16[1024,512]{1,0:T(8,128)(2,1)}, ...) | async-done | bytes 4194320 | tf_op jit(solution)/shard_map/psum | solution.py:249
  593.4 4.3 fusion.131
  597.6 156.5 %reduce-scatter.14.cloned.1.call-done = bf16[64,4224]{1,0:T(8,128)(2,1)} async-done(((bf16[1024,4224]{1,0:T(8,128)(2,1)}), bf16[64,4224]{1,0:T(8,128)(2,1)}) %reduce-scatter.14.cloned.1.call-update) | async-done | bytes 540688 | tf_op jit(solution)/shard_map/reduce_scatter | solution.py:211
  757.0 9.0 %reduce_sum.79 = bf16[1024,512]{1,0:T(8,128)(2,1)S(1)} reduce(bf16[16,1024,512]{2,1,0:T(8,128)(2,1)} %bitcast.254, bf16[]{:T(256)} %constant.119.clone.1), dimensions={0}, to_apply=%region_16.17 | reduce | flops 7864320 | bytes 17825794 | tf_op jit(solution)/shard_map/reduce_sum | solution.py:246
  (244 shorter events, 147.7 us)
Async XLA Ops:
  8.0 95.1 %copy-start = (bf16[512,1024]{1,0:T(8,128)(2,1)S(1)}, bf16[512,1024]{1,0:T(8,128)(2,1)}, u32[]{:S(2)}) copy-start(bf16[512,1024]{1,0:T(8,128)(2,1)} %param.23) | copy-start | bytes 3145732
  8.0 40.8 %all-gather.10.cloned.1.call-start = ((), (), s32[]{:S(2)}) async-start(), calls=%async_computation.5 | async-start | bytes 3145728 | tf_op jit(solution)/shard_map/all_gather | solution.py:163
  8.1 4.8 copy-start.52
  10.3 38.5 %copy-start.48 = (bf16[1024,512]{1,0:T(8,128)(2,1)S(1)}, bf16[1024,512]{1,0:T(8,128)(2,1)}, u32[]{:S(2)}) copy-start(bf16[1024,512]{1,0:T(8,128)(2,1)} %param.20) | copy-start | bytes 3145732
  12.8 125.0 %reduce-scatter.6.cloned.1.call-start = ((), (), s32[]{:S(2)}) async-start(), calls=%async_computation.6 | async-start | bytes 3145728 | tf_op jit(solution)/shard_map/reduce_scatter | solution.py:177
  72.1 3.7 copy-start.13
  79.7 3.7 copy-start.13
  84.2 6.3 copy-start.6
  92.5 9.6 %copy-start.4 = (f32[64,8,2,512]{3,1,2,0:T(8,128)}, f32[64,8,2,512]{3,1,2,0:T(8,128)S(1)}, u32[]{:S(2)}) copy-start(f32[64,8,2,512]{3,1,2,0:T(8,128)S(1)} %copy.52) | copy-start | bytes 6291460
  105.8 32.0 %copy-start.2 = (bf16[512,1024]{1,0:T(8,128)(2,1)S(1)}, bf16[512,1024]{1,0:T(8,128)(2,1)}, u32[]{:S(2)}) copy-start(bf16[512,1024]{1,0:T(8,128)(2,1)} %param.16) | copy-start | bytes 3145732
  105.8 47.0 %all-gather.14.cloned.1.call-start = ((), (), s32[]{:S(2)}) async-start(), calls=%async_computation.8 | async-start | bytes 3063808 | tf_op jit(solution)/shard_map/all_gather | solution.py:184
  106.4 80.2 %all-gather.12.cloned.1.call-start = ((), (), s32[]{:S(2)}) async-start(), calls=%async_computation.7 | async-start | bytes 3145728 | tf_op jit(solution)/shard_map/all_gather | solution.py:182
  140.8 92.1 %all-gather.16.cloned.1.call-start = ((), (), s32[]{:S(2)}) async-start(), calls=%async_computation.9 | async-start | bytes 3063808 | tf_op jit(solution)/shard_map/all_gather | solution.py:185
  141.4 125.4 %all-gather.20.cloned.1.call-start = ((), (), s32[]{:S(2)}) async-start(), calls=%async_computation.12 | async-start | bytes 3145728 | tf_op jit(solution)/shard_map/all_gather | solution.py:196
  144.6 168.8 %all-gather.18.cloned.1.call-start = ((), (), s32[]{:S(2)}) async-start(), calls=%async_computation.10 | async-start | bytes 3063808 | tf_op jit(solution)/shard_map/all_gather | solution.py:187
  145.3 218.3 %reduce-scatter.10.cloned.1.call-start = ((), (), s32[]{:S(2)}) async-start(), calls=%async_computation.13 | async-start | bytes 3145728 | tf_op jit(solution)/shard_map/reduce_scatter | solution.py:200
  313.4 11.0 %copy-start.45 = (bf16[1024,1408]{1,0:T(8,128)(2,1)S(1)}, bf16[1024,1408]{1,0:T(8,128)(2,1)}, u32[]{:S(2)}) copy-start(bf16[1024,1408]{1,0:T(8,128)(2,1)} %all-gather.14.cloned.1.call-done) | copy-start | bytes 8650756
  324.4 3.9 copy-start.46
  333.0 67.8 %all-gather.22.cloned.1.call-start = ((), (), s32[]{:S(2)}) async-start(), calls=%async_computation.14 | async-start | bytes 3145728 | tf_op jit(solution)/shard_map/all_gather | solution.py:222
  367.5 33.3 %copy-start.5 = (f32[64,8,2,512]{3,1,2,0:T(8,128)S(1)}, f32[64,8,2,512]{3,1,2,0:T(8,128)}, u32[]{:S(2)}) copy-start(f32[64,8,2,512]{3,1,2,0:T(8,128)} %copy-done.4) | copy-start | bytes 6291460
  367.5 216.0 %all-reduce.3.cloned.1.call-start = ((), (), s32[]{:S(2)}) async-start(), calls=%async_computation.18 | async-start | bytes 8388608 | tf_op jit(solution)/shard_map/psum | solution.py:249
  426.3 3.7 copy-start.8
  444.6 3.7 copy-start.8
  444.6 3.7 copy-start.10
  471.5 119.9 %reduce-scatter.12.cloned.1.call-start = ((), (), s32[]{:S(2)}) async-start(), calls=%async_computation.15 | async-start | bytes 3145728 | tf_op jit(solution)/shard_map/reduce_scatter | solution.py:236
  484.8 108.5 %reduce-scatter.8.cloned.1.call-start = ((), (), s32[]{:S(2)}) async-start(), calls=%async_computation.11 | async-start | bytes 3145728 | tf_op jit(solution)/shard_map/reduce_scatter | solution.py:191
  492.4 261.8 %reduce-scatter.14.cloned.1.call-start = ((), (), s32[]{:S(2)}) async-start(), calls=%async_computation.16 | async-start | bytes 9191424 | tf_op jit(solution)/shard_map/reduce_scatter | solution.py:211
  494.0 5.7 copy-start.27
  494.0 5.7 copy-start.29
  494.0 5.7 copy-start.47
  510.4 246.6 %all-gather.24.cloned.1.call-start = ((), (), s32[]{:S(2)}) async-start(), calls=%async_computation.17 | async-start | bytes 17825792 | tf_op jit(solution)/shard_map/all_gather | solution.py:247
  757.0 10.6 %copy-start.1 = (bf16[512,1024]{1,0:T(8,128)(2,1)S(1)}, bf16[512,1024]{1,0:T(8,128)(2,1)}, u32[]{:S(2)}) copy-start(bf16[512,1024]{1,0:T(8,128)(2,1)} %param.23) | copy-start | bytes 3145732
  (43 other events, 92.0 us)
Sparse Core Ops, SparseCore 0:
  12.9 35.8 all-gather.9
  105.9 31.7 reduce-scatter.5
  333.1 30.4 reduce-scatter.9
  367.6 33.0 all-gather.21
  484.9 32.1 reduce-scatter.11
  519.9 31.8 reduce-scatter.7
  556.4 197.6 reduce-scatter.13
Sparse Core Ops, SparseCore 1:
  108.8 43.9 all-gather.13
  154.9 31.6 all-gather.11
  189.0 43.9 all-gather.15
  235.2 31.6 all-gather.19
  269.4 43.9 all-gather.17
  471.6 111.8 all-reduce.2
  585.8 164.5 all-gather.23
